TPU v7x, 256 devices: a whole 4x4x8 slice. The times are simulated.
256 devices in a mesh: samp: 64 (over z_lo, x, y, core), var: 4 (over z_hi).
Axes of the slice: x: 4, y: 4, z: 8 (z_hi: 4, z_lo: 2; z = z_hi * 2 + z_lo), core: 2. Of those that a mesh axis runs over, the one named last changes fastest.
Arguments:
- genotypes: bfloat16 [65536, 16384], P('samp', 'var'), may hold values from 0 to 2, as said below
- col_mean: float32 [16384], P('var'), may hold values from 0.1 to 1, as said below
- inv_scale: float32 [16384], P('var'), may hold values from 1.4 to 3.25, as said below
- targets: float32 [65536], P('samp'), may hold values from -6 to 6
- probes: float32 [65536, 7], P('samp'), may hold values from -6 to 6
- delta: float32 [1], replicated, may hold values from 0.5 to 2
Outputs:
- solution: float32 [65536, 8], P('samp')
- assoc: float32 [16384], P('var')
Inputs may be any that keep to these rules, and one draw needn't show every extreme that they name: `genotypes`: dosages 0, 1 or 2, drawn per variant from an allele frequency f of 0.05 to 0.5. `col_mean`: 2 f for the variant's allele frequency f. `inv_scale`: 1 / sqrt(2 f (1 - f)) for the same frequency f.
All inputs are finite; a program needn't handle non-finite values.
Results may differ from a plain program's by a relative error of at most 0.0003.
Values sent between devices are 32-bit elements; how exact they have to be, the bound alone decides.
A program may use at most 64 MiB of HBM per device.

v0:
```python
import jax
import jax.numpy as jnp
from jax import lax
from jax.sharding import PartitionSpec as P

ITERS = 2


HI = lax.Precision.HIGHEST


def split_up(shard, dim, count):
    dims = shard.shape
    tiles = shard.reshape(*dims[:dim], count, dims[dim] // count, *dims[dim + 1 :])
    return jnp.moveaxis(tiles, dim, 0)


def sent_and_summed(shard, axis, dim):
    tiles = split_up(shard, dim, lax.axis_size(axis))
    arrived = lax.all_to_all(tiles, axis, split_axis=0, concat_axis=0, tiled=True)
    return arrived.sum(axis=0)


def from_everyone(shard, axis):
    count = lax.axis_size(axis)
    return lax.all_to_all(
        jnp.broadcast_to(shard[None], (count, *shard.shape)), axis, 0, 0, tiled=True
    )


def over_copies(shard, axis):
    return from_everyone(shard, axis).sum(axis=0)


def packed_total(arrays, axis):
    flat, at, outs = (jnp.concatenate([a.reshape(-1) for a in arrays]), 0, [])
    so_far = over_copies(flat, axis)
    for a in arrays:
        outs.append(so_far[at : at + a.size].reshape(a.shape))
        at += a.size
    return tuple(outs)


def in_order(tiles, dim):
    dims = list(tiles.shape[1:])
    dims[dim] *= tiles.shape[0]
    return jnp.moveaxis(tiles, 0, dim).reshape(dims)


def gathered_copies(shard, axis, dim):
    return in_order(from_everyone(shard, axis), dim)


def per_device(genotypes, col_mean, inv_scale, targets, probes, delta):
    n_total = genotypes.shape[0] * lax.axis_size("samp")
    m_total = genotypes.shape[1] * lax.axis_size("var")
    shift = delta[0]
    dense = genotypes.astype(jnp.float32)
    rhs = jnp.concatenate([targets[:, None], probes], 1)

    def transposed(vectors):
        return lax.dot_general(
            dense,
            vectors,
            (((0,), (0,)), ((), ())),
            precision=HI,
            preferred_element_type=jnp.float32,
        )

    def across(vectors, other):
        part = transposed(vectors)
        totals = jnp.sum(vectors, 0)
        squares = jnp.sum(vectors * vectors, 0)
        inner = jnp.sum(vectors * other, 0)
        share = sent_and_summed(part, "samp", 0)
        totals, squares, inner = packed_total((totals, squares, inner), "samp")
        width = share.shape[0]
        start = lax.axis_index("samp") * width
        mean_part = lax.dynamic_slice_in_dim(col_mean, start, width)
        inv_part = lax.dynamic_slice_in_dim(inv_scale, start, width)
        finished = inv_part[:, None] * (share - mean_part[:, None] * totals[None, :])
        return (gathered_copies(finished, "samp", 0), squares, inner)

    solution = jnp.zeros_like(rhs)
    residual = rhs
    direction = rhs
    nothing = jnp.zeros_like(rhs)
    columns = None
    norm_now = None
    dir_squares = None
    for step in range(ITERS):
        if step == 0:
            columns, res_squares, inner = across(residual, nothing)
            direction = residual
            dir_squares = res_squares
        else:
            res_columns, res_squares, inner = across(residual, direction)
            beta = res_squares / norm_now
            direction = residual + beta[None, :] * direction
            columns = res_columns + beta[None, :] * columns
            dir_squares = res_squares + 2.0 * beta * inner + beta * beta * dir_squares
        norm_now = res_squares
        scaled = inv_scale[:, None] * columns
        offset = jnp.dot(col_mean, scaled, precision=HI, preferred_element_type=jnp.float32)
        partial_value = (
            jnp.dot(dense, scaled, precision=HI, preferred_element_type=jnp.float32)
            - offset[None, :]
        )
        summed, column_squares = packed_total((partial_value, jnp.sum(columns * columns, 0)), "var")
        image = summed / m_total + shift * direction
        curving = column_squares / m_total + shift * dir_squares
        image, curving = (image, curving)
        alpha = norm_now / curving
        solution = solution + alpha[None, :] * direction
        if step + 1 < ITERS:
            residual = residual - alpha[None, :] * image
    target_sol = solution[:, 0:1]
    part = transposed(target_sol)[:, 0]
    part, total = packed_total((part, jnp.sum(target_sol)), "samp")
    first = inv_scale * (part - col_mean * total)
    assoc = first / jnp.sqrt(jnp.float32(n_total))
    return (solution, assoc)


def solution(mesh):
    placed = (P("samp", "var"), P("var"), P("var"), P("samp"), P("samp", None), P())
    return jax.shard_map(
        per_device,
        mesh=mesh,
        in_specs=placed,
        out_specs=(P("samp", None), P("var")),
        check_vma=False,
    )
```

profile of v0, /device:TPU:1, one launch (start us, length us, event | category | flops | bytes accessed | tf_op | source)
XLA Modules:
  0.0 179.3 jit_solution(4110416892408576758)
XLA Ops:
  0.6 0.9 fusion.14
  1.7 0.6 broadcast_in_dim.20
  2.3 10.3 %all-to-all-start = ((f32[64,1,24]{2,1,0:T(1,128)}), f32[64,1,24]{2,1,0:T(1,128)S(1)}, u32[]{:S(2)}, u32[]{:S(2)}) async-start(f32[64,1,24]{2,1,0:T(1,128)} %broadcast_in_dim.20), calls=%async_computation | async-start | bytes 65536 | tf_op jit(solution)/shard_map/all_to_all | solution.py:26
  12.6 5.7 %convolution_bitcast_fusion.1 = f32[4096,8]{0,1:T(8,128)S(1)} fusion(bf16[1024,4096]{1,0:T(8,128)(2,1)} %param.6, f32[1024,7]{0,1:T(8,128)} %param.10, f32[1024,1]{0,1:T(1,128)} %bitcast.67), kind=kOutput, calls=%fused_computation.1 | convolution fusion | flops 402661376 | bytes 8552448 | tf_op jit(solution)/shard_map/dot_general | solution.py:62
  18.6 0.8 reshape.179
  19.4 1.0 all-to-all-done
  20.4 7.9 %all-to-all-start.1 = ((f32[64,1,512]{2,1,0:T(1,128)}), f32[64,1,512]{2,1,0:T(1,128)S(1)}, u32[]{:S(2)}, u32[]{:S(2)}) async-start(f32[64,1,512]{2,1,0:T(1,128)} %reshape.179), calls=%async_computation.1 | async-start | bytes 262144 | tf_op jit(solution)/shard_map/all_to_all | solution.py:20
  28.6 8.2 %all-to-all-done.1 = f32[64,1,512]{2,1,0:T(1,128)S(1)} async-done(((f32[64,1,512]{2,1,0:T(1,128)}), f32[64,1,512]{2,1,0:T(1,128)S(1)}, u32[]{:S(2)}, u32[]{:S(2)}) %all-to-all-start.1) | async-done | bytes 131104 | tf_op jit(solution)/shard_map/all_to_all | solution.py:20
  36.8 0.5 broadcast.97
  37.3 0.9 reduce.7
  38.6 0.2 reshape.181
  38.7 12.5 %all_to_all.50 = f32[64,1,512]{2,1,0:T(1,128)S(1)} all-to-all(f32[64,1,512]{2,1,0:T(1,128)S(1)} %reshape.181), channel_id=1, replica_groups=mesh['samp'=64,'var'=4] {'samp'}, dimensions={0} | all-to-all | bytes 262144 | tf_op jit(solution)/shard_map/all_to_all | solution.py:26
  51.3 1.0 reduce.8
  52.3 0.2 multiply_reduce_fusion.1
  52.7 0.4 convolution_bitcast_fusion.3
  53.1 8.9 %fusion.1 = f32[1024,8]{0,1:T(8,128)S(1)} fusion(bf16[1024,4096]{1,0:T(8,128)(2,1)} %param.6, f32[4096,8]{0,1:T(8,128)S(1)} %reshape.165, f32[4096]{0:T(1024)S(1)} %copy-done.1, f32[8]{0:T(128)S(1)} %convolution_bitcast_fusion.3), kind=kOutput, calls=%fused_computation.5 | convolution fusion | flops 402694144 | bytes 8568864 | tf_op jit(solution)/shard_map/dot_general | solution.py:106
  62.0 0.2 copy.92
  62.2 0.3 reshape.166
  62.5 0.7 broadcast_in_dim.22
  63.2 7.3 %all-to-all-start.3 = ((f32[4,1,8200]{2,1,0:T(1,128)}), f32[4,1,8200]{2,1,0:T(1,128)S(1)}, u32[]{:S(2)}, u32[]{:S(2)}) async-start(f32[4,1,8200]{2,1,0:T(1,128)} %broadcast_in_dim.22), calls=%async_computation.3 | async-start | bytes 266240 | tf_op jit(solution)/shard_map/all_to_all | solution.py:26
  71.1 6.8 %all-to-all-done.3 = f32[4,1,8200]{2,1,0:T(1,128)S(1)} async-done(((f32[4,1,8200]{2,1,0:T(1,128)}), f32[4,1,8200]{2,1,0:T(1,128)S(1)}, u32[]{:S(2)}, u32[]{:S(2)}) %all-to-all-start.3) | async-done | bytes 131232 | tf_op jit(solution)/shard_map/all_to_all | solution.py:26
  78.1 0.3 div.33
  78.6 0.2 fusion.15
  78.9 0.6 broadcast_in_dim.23
  79.5 6.5 %all-to-all-start.4 = ((f32[64,1,24]{2,1,0:T(1,128)}), f32[64,1,24]{2,1,0:T(1,128)S(1)}, u32[]{:S(2)}, u32[]{:S(2)}) async-start(f32[64,1,24]{2,1,0:T(1,128)} %broadcast_in_dim.23), calls=%async_computation.4 | async-start | bytes 65536 | tf_op jit(solution)/shard_map/all_to_all | solution.py:26
  86.1 5.7 %convolution_bitcast_fusion = f32[4096,8]{0,1:T(8,128)S(1)} fusion(f32[1024,8]{0,1:T(8,128)S(1)} %get-tuple-element.20, bf16[1024,4096]{1,0:T(8,128)(2,1)} %param.6), kind=kOutput, calls=%fused_computation | convolution fusion | flops 402653184 | bytes 8552448 | tf_op jit(solution)/shard_map/dot_general | solution.py:62
  92.0 0.8 reshape.183
  92.8 1.1 all-to-all-done.4
  93.9 7.9 %all-to-all-start.5 = ((f32[64,1,512]{2,1,0:T(1,128)}), f32[64,1,512]{2,1,0:T(1,128)S(1)}, u32[]{:S(2)}, u32[]{:S(2)}) async-start(f32[64,1,512]{2,1,0:T(1,128)} %reshape.183), calls=%async_computation.5 | async-start | bytes 262144 | tf_op jit(solution)/shard_map/all_to_all | solution.py:20
  102.0 8.3 %all-to-all-done.5 = f32[64,1,512]{2,1,0:T(1,128)S(1)} async-done(((f32[64,1,512]{2,1,0:T(1,128)}), f32[64,1,512]{2,1,0:T(1,128)S(1)}, u32[]{:S(2)}, u32[]{:S(2)}) %all-to-all-start.5) | async-done | bytes 131104 | tf_op jit(solution)/shard_map/all_to_all | solution.py:20
  110.3 1.0 reduce.9
  111.5 0.2 reshape.185
  111.7 12.5 %all_to_all.51 = f32[64,1,512]{2,1,0:T(1,128)S(1)} all-to-all(f32[64,1,512]{2,1,0:T(1,128)S(1)} %reshape.185), channel_id=1, replica_groups=mesh['samp'=64,'var'=4] {'samp'}, dimensions={0} | all-to-all | bytes 262144 | tf_op jit(solution)/shard_map/all_to_all | solution.py:26
  124.2 1.0 reduce.10
  125.3 0.3 multiply_reduce_fusion
  125.7 0.4 convolution_bitcast_fusion.2
  126.1 8.9 %fusion = f32[1024,8]{0,1:T(8,128)S(1)} fusion(bf16[1024,4096]{1,0:T(8,128)(2,1)} %param.6, f32[8]{0:T(128)S(1)} %convolution_bitcast_fusion.2, f32[4096,8]{0,1:T(8,128)S(1)} %reshape.168, f32[4096,8]{0,1:T(8,128)S(1)} %reshape.165, f32[8]{0:T(128)S(1)} %get-tuple-element.22, f32[4096]{0:T(1024)S(1)} %copy-done.1), kind=kOutput, calls=%fused_computation.3 | convolution fusion | flops 402759680 | bytes 8699968 | tf_op jit(solution)/shard_map/dot_general | solution.py:106
  135.1 0.2 copy.99
  135.3 0.3 reshape.169
  135.7 9.8 %all_to_all.52 = f32[4,1,8200]{2,1,0:T(1,128)S(1)} all-to-all(f32[4,1,8200]{2,1,0:T(1,128)S(1)} %broadcast_in_dim.25), channel_id=1, replica_groups=mesh['samp'=64,'var'=4] {'var'}, dimensions={0} | all-to-all | bytes 262400 | tf_op jit(solution)/shard_map/all_to_all | solution.py:26
  145.8 0.6 slice_reduce_fusion
  146.4 5.7 %fusion.8 = f32[1,4096]{1,0:T(1,128)S(1)} fusion(bf16[1024,4096]{1,0:T(8,128)(2,1)} %param.6, f32[1024,8]{0,1:T(8,128)S(1)} %multiply_add_fusion), kind=kOutput, calls=%fused_computation.32 | convolution fusion | flops 50331648 | bytes 8409088 | tf_op jit(solution)/shard_map/dot_general | solution.py:62
  152.0 0.7 pad_maximum_fusion.3
  152.7 0.6 broadcast_in_dim.26
  153.3 23.4 %all_to_all.53 = f32[64,1,4097]{2,1,0:T(1,128)S(1)} all-to-all(f32[64,1,4097]{2,1,0:T(1,128)S(1)} %broadcast_in_dim.26), channel_id=1, replica_groups=mesh['samp'=64,'var'=4] {'samp'}, dimensions={0} | all-to-all | bytes 2097664 | tf_op jit(solution)/shard_map/all_to_all | solution.py:26
  176.7 0.7 reduce_sum.159
  177.4 0.6 slice.57
  178.0 1.3 fusion.7
  (45 shorter events, 2.9 us)
Async XLA Ops:
  0.6 27.7 %copy-start.3 = (f32[4096]{0:T(1024)S(1)}, f32[4096]{0:T(1024)}, u32[]{:S(2)}) copy-start(f32[4096]{0:T(1024)} %param.7) | copy-start | bytes 49156
  0.6 27.8 %copy-start.1 = (f32[4096]{0:T(1024)S(1)}, f32[4096]{0:T(1024)}, u32[]{:S(2)}) copy-start(f32[4096]{0:T(1024)} %param.8) | copy-start | bytes 49156
  2.3 18.1 %all-to-all-start = ((f32[64,1,24]{2,1,0:T(1,128)}), f32[64,1,24]{2,1,0:T(1,128)S(1)}, u32[]{:S(2)}, u32[]{:S(2)}) async-start(f32[64,1,24]{2,1,0:T(1,128)} %broadcast_in_dim.20), calls=%async_computation | async-start | bytes 65536 | tf_op jit(solution)/shard_map/all_to_all | solution.py:26
  18.4 60.2 %copy-start = (f32[1024,7]{0,1:T(8,128)S(1)}, f32[1024,7]{0,1:T(8,128)}, u32[]{:S(2)}) copy-start(f32[1024,7]{0,1:T(8,128)} %param.10) | copy-start | bytes 86020
  18.4 60.2 %copy-start.4 = (f32[1024]{0:T(1024)S(1)}, f32[1024]{0:T(1024)}, u32[]{:S(2)}) copy-start(f32[1024]{0:T(1024)} %param.9) | copy-start | bytes 12292
  20.4 16.4 %all-to-all-start.1 = ((f32[64,1,512]{2,1,0:T(1,128)}), f32[64,1,512]{2,1,0:T(1,128)S(1)}, u32[]{:S(2)}, u32[]{:S(2)}) async-start(f32[64,1,512]{2,1,0:T(1,128)} %reshape.179), calls=%async_computation.1 | async-start | bytes 262144 | tf_op jit(solution)/shard_map/all_to_all | solution.py:20
  63.2 14.7 %all-to-all-start.3 = ((f32[4,1,8200]{2,1,0:T(1,128)}), f32[4,1,8200]{2,1,0:T(1,128)S(1)}, u32[]{:S(2)}, u32[]{:S(2)}) async-start(f32[4,1,8200]{2,1,0:T(1,128)} %broadcast_in_dim.22), calls=%async_computation.3 | async-start | bytes 266240 | tf_op jit(solution)/shard_map/all_to_all | solution.py:26
  79.5 14.4 %all-to-all-start.4 = ((f32[64,1,24]{2,1,0:T(1,128)}), f32[64,1,24]{2,1,0:T(1,128)S(1)}, u32[]{:S(2)}, u32[]{:S(2)}) async-start(f32[64,1,24]{2,1,0:T(1,128)} %broadcast_in_dim.23), calls=%async_computation.4 | async-start | bytes 65536 | tf_op jit(solution)/shard_map/all_to_all | solution.py:26
  93.9 16.3 %all-to-all-start.5 = ((f32[64,1,512]{2,1,0:T(1,128)}), f32[64,1,512]{2,1,0:T(1,128)S(1)}, u32[]{:S(2)}, u32[]{:S(2)}) async-start(f32[64,1,512]{2,1,0:T(1,128)} %reshape.183), calls=%async_computation.5 | async-start | bytes 262144 | tf_op jit(solution)/shard_map/all_to_all | solution.py:20
  145.8 31.0 %copy-start.2 = (f32[1024,8]{0,1:T(8,128)}, f32[1024,8]{0,1:T(8,128)S(1)}, u32[]{:S(2)}) copy-start(f32[1024,8]{0,1:T(8,128)S(1)} %multiply_add_fusion) | copy-start | bytes 98308
where the time goes:
time: 180 us; the launch traced here: 179 us
  blocking collectives  58.3 us (32%)
  starting transfers between devices  39.9 us (22%)
  matrix products  35.7 us (20%)
  waiting for transfers between devices  25.4 us (14%)
  other arithmetic  9.81 us (5%)
  local copies, waits for them, and re-layouts  8.61 us (5%)
    all_to_all x4, blocking collectives, from_everyone(): lax.all_to_all(jnp.broadcast_to(shard[None], (count, *shard.shape)), axis...  58.3 us
    all_to_all x3, starting transfers between devices, from_everyone(): lax.all_to_all(jnp.broadcast_to(shard[None], (count, *shard.shape)), axis...  24.1 us
    dot_general x2, matrix products, per_device(): jnp.dot(dense, scaled, precision=HI, preferred_element_type=jnp.float32)  17.9 us
    dot_general x3, matrix products, transposed(): lax.dot_general(dense, vectors, (((0,), (0,)), ((), ())), precision=HI, p...  17 us
    all_to_all x2, waiting for transfers between devices, sent_and_summed(): lax.all_to_all(tiles, axis, split_axis=0, concat_axis=0, tiled=True)  16.5 us
    all_to_all x2, starting transfers between devices, sent_and_summed(): lax.all_to_all(tiles, axis, split_axis=0, concat_axis=0, tiled=True)  15.8 us
    all_to_all x3, waiting for transfers between devices, from_everyone(): lax.all_to_all(jnp.broadcast_to(shard[None], (count, *shard.shape)), axis...  8.9 us
  transfers between devices with their start and end apart: 5, of which 5 were waited for; matrix products, arithmetic and copies ran while one was open for 8% of the time, Pallas kernels for 0%

commit v1 on v0

v1 whole, which is shorter than its diff:
```python
import functools
import math

import jax
import jax.numpy as jnp
from jax import lax
from jax.experimental import pallas as pl
from jax.experimental.pallas import tpu as pltpu
from jax.sharding import PartitionSpec as P

MESH = pl.DeviceIdType.MESH
PLACES = (2, 4, 4, 2)
COLS = 8
LANES = 128


def far(a, n):
    if n == 4:
        return lax.rem(2 + 3 * a + 3 * ((a * (a - 1)) // 2), 4)
    return n - 1 - a


def three(v):
    high = v.astype(jnp.bfloat16).astype(jnp.float32)
    rest = v - high
    mid = rest.astype(jnp.bfloat16).astype(jnp.float32)
    low = rest - mid
    return jnp.concatenate([high, mid, low], 0).astype(jnp.bfloat16)


def folded(p):
    return p[0:COLS] + p[COLS : 2 * COLS] + p[2 * COLS : 3 * COLS]


def kernel(
    places, n_var, n_total, m_total,
    g_hbm, mean_ref, inv_ref, target_ref, probe_ref, delta_ref,
    sol_ref, assoc_ref,
    g_ref, rhs_ref, send1, recv1, c0_ref, part_ref, send2, recv2, sums_ref, z_ref,
    g_sem, rs_send, rs_recv, ag_send, ag_recv, var_sem, sum_send, sum_recv, z_sem,
):
    n_zl, n_x, n_y, n_core = places
    n_samp = n_zl * n_x * n_y * n_core
    plane = n_x * n_y * n_core
    members = n_y * n_core
    half = COLS // n_core
    width = n_y * LANES
    n_z = n_var * n_zl
    me = lax.axis_index("samp")
    va = lax.axis_index("var")
    core = lax.rem(me, n_core)
    y = lax.rem(me // n_core, n_y)
    x = lax.rem(me // members, n_x)
    zl = me // plane
    z = va * n_zl + zl
    mine = me // members
    in_plane = lax.rem(me, plane)
    offsets = [(dz, dx) for dz in range(n_zl) for dx in range(n_x)]
    near_first = sorted(offsets, key=lambda o: (o[0] + min(o[1], n_x - o[1]), o))
    far_first = near_first[::-1]

    def group_of(o):
        return lax.rem(zl + o[0], n_zl) * n_x + lax.rem(x + o[1], n_x)

    def each_member(o, act):
        group = group_of(o)

        def one(k, carry):
            ty = lax.rem(y + far(k // n_core, n_y), n_y)
            tc = lax.rem(core + n_core - 1 - lax.rem(k, n_core), n_core)
            act(group * members + ty * n_core + tc)
            return carry

        lax.fori_loop(0, members - (1 if o == (0, 0) else 0), one, 0)

    def to(src, dst, send, recv, samp, var):
        pltpu.make_async_remote_copy(
            src_ref=src, dst_ref=dst, send_sem=send, recv_sem=recv, device_id=(samp, var), device_id_type=MESH
        ).start()

    def arrived(ref, count, sem):
        some = ref.at[pl.ds(0, count)]
        pltpu.make_async_copy(some, some, sem).wait()

    def block(i, group):
        columns = pl.ds(pl.multiple_of(group * width, width), width)
        return pltpu.make_async_copy(g_hbm.at[:, columns], g_ref.at[group], g_sem.at[i])

    for i, o in enumerate(far_first):
        block(i, group_of(o)).start()

    barrier = pltpu.get_barrier_semaphore()

    def greet(k, carry):
        pl.semaphore_signal(barrier, inc=1, device_id=(lax.rem(me + k, n_samp), va), device_id_type=MESH)
        return carry

    lax.fori_loop(1, n_samp, greet, 0)

    def on_line(d):
        tz = lax.rem(z + d, n_z)
        return lax.rem(tz, n_zl) * plane + in_plane, tz // n_zl

    for d in range(1, n_z):
        pl.semaphore_signal(barrier, inc=1, device_id=on_line(d), device_id_type=MESH)

    rhs_ref[0:1, :] = target_ref[...]
    rhs_ref[1:COLS, :] = probe_ref[...]
    rhs = rhs_ref[...]

    def reduced(vec, send, recv, sem, first):
        pieces = three(vec)
        total = jnp.sum(vec, 1, keepdims=True)
        before = None
        for i, o in enumerate(far_first):
            group = group_of(o)
            if first:
                block(i, group).wait()
            p = folded(jnp.dot(pieces, g_ref[group], preferred_element_type=jnp.float32))
            p = p - total * mean_ref[group]
            for ky in range(n_y):
                for kc in range(n_core):
                    send[group * members + ky * n_core + kc] = p[
                        kc * half : (kc + 1) * half, ky * LANES : (ky + 1) * LANES
                    ]
            if first and i == 0:
                pl.semaphore_wait(barrier, n_samp - 1 + n_z - 1)
            if before is not None:
                each_member(
                    before, lambda t: to(send.at[t], recv.at[me], rs_send.at[sem], rs_recv.at[sem], t, va)
                )
            before = o
        each_member(before, lambda t: to(send.at[t], recv.at[me], rs_send.at[sem], rs_recv.at[sem], t, va))
        recv[me] = send[me]
        arrived(recv, n_samp - 1, rs_recv.at[sem])
        scale = inv_ref[mine, :, pl.ds(pl.multiple_of(y * LANES, LANES), LANES)]
        return jnp.sum(recv[...], 0) * scale

    share0 = reduced(rhs, send1, recv1, 0, True)
    c0_ref[me] = share0
    for o in far_first:
        each_member(o, lambda t: to(c0_ref.at[me], c0_ref.at[me], ag_send, ag_recv.at[mine], t, va))

    rows = None
    shift = None
    for o in near_first:
        group = group_of(o)
        arrived(c0_ref, members - (1 if o == (0, 0) else 0), ag_recv.at[group])
        blocks = []
        for ky in range(n_y):
            blocks.append(
                jnp.concatenate([c0_ref[group * members + ky * n_core + kc] for kc in range(n_core)], 0)
            )
        scaled = jnp.concatenate(blocks, 1) * inv_ref[group]
        off = jnp.sum(scaled * mean_ref[group], 1, keepdims=True)
        p = lax.dot_general(
            three(scaled), g_ref[group], (((1,), (1,)), ((), ())), preferred_element_type=jnp.float32
        )
        rows = p if rows is None else rows + p
        shift = off if shift is None else shift + off
    part_ref[va] = folded(rows) - shift
    for d in sorted(range(1, n_var), key=lambda d: -min(d, n_var - d)):
        to(part_ref.at[va], part_ref.at[va], var_sem.at[0], var_sem.at[1], me, lax.rem(va + d, n_var))
    arrived(part_ref, n_var - 1, var_sem.at[1])
    image = part_ref[0]
    for k in range(1, n_var):
        image = image + part_ref[k]
    image = image * (1.0 / m_total)

    share1 = reduced(image, send2, recv2, 1, False)

    row = lax.broadcasted_iota(jnp.int32, (COLS, LANES), 0)
    lane = lax.broadcasted_iota(jnp.int32, (COLS, LANES), 1)
    own = row // half == core

    def by_column(a):
        spread = jnp.where(own, jnp.concatenate([a] * n_core, 0), 0.0)
        return jnp.sum(spread, 1, keepdims=True)

    def by_sample(a):
        return jnp.sum(a, 1, keepdims=True) * (1.0 / n_var)

    found = [
        by_column(share0 * share0), by_column(share0 * share1), by_column(share1 * share1),
        by_sample(rhs * rhs), by_sample(rhs * image), by_sample(image * image),
    ]
    spread = jnp.zeros((COLS, LANES), jnp.float32)
    for k, q in enumerate(found):
        spread = jnp.where(lane == row + COLS * k, q, spread)
    sums_ref[me] = jnp.concatenate([jnp.sum(spread, 0, keepdims=True), share1[0:1, :]], 0)
    for o in sorted(far_first, key=lambda o: o[0]):
        each_member(o, lambda t: to(sums_ref.at[me], sums_ref.at[me], sum_send, sum_recv.at[zl], t, va))
    arrived(sums_ref, plane - 1, sum_recv.at[zl])
    z_ref[z] = jnp.sum(sums_ref[pl.ds(zl * plane, plane)], 0)[0:1, :]
    for d in sorted(range(1, n_z), key=lambda d: -min(d, n_z - d)):
        to(z_ref.at[z], z_ref.at[z], z_sem.at[0], z_sem.at[1], *on_line(d))
    for other in range(1, n_zl):
        arrived(sums_ref, plane, sum_recv.at[lax.rem(zl + other, n_zl)])
    arrived(z_ref, n_z - 1, z_sem.at[1])
    every = jnp.broadcast_to(jnp.sum(z_ref[...], 0), (COLS, LANES))
    cc, cw, ww, rr, ri, ii = [
        jnp.sum(jnp.where(lane == row + COLS * k, every, 0.0), 1, keepdims=True) for k in range(len(found))
    ]

    delta = delta_ref[0]
    slope = ri / rr
    alpha0 = rr / (ri + delta * rr)
    norm1 = alpha0 * alpha0 * (ii - slope * ri)
    beta = norm1 / rr
    lead = alpha0 * slope + beta
    across = lead * lead * cc - 2.0 * lead * alpha0 * cw + alpha0 * alpha0 * ww
    alpha1 = norm1 / (across * (1.0 / m_total) + delta * (norm1 + beta * beta * rr))
    keep = alpha0 + alpha1 * lead
    less = alpha1 * alpha0
    sol_ref[...] = keep * rhs - less * image
    root = 1.0 / math.sqrt(n_total)
    keep_row = jnp.broadcast_to(keep[0:1, 0:1] * root, (1, LANES))
    less_row = jnp.broadcast_to(less[0:1, 0:1] * root, (1, LANES))
    for q in range(n_samp // n_core):
        at = q * n_core
        assoc_ref[q] = keep_row * c0_ref[at, 0:1, :] - less_row * sums_ref[at, 1:2, :]

    arrived(send1, n_samp - 1, rs_send.at[0])
    arrived(c0_ref, n_samp - 1, ag_send)
    arrived(part_ref, n_var - 1, var_sem.at[0])
    arrived(send2, n_samp - 1, rs_send.at[1])
    arrived(sums_ref, n_samp - 1, sum_send)
    arrived(z_ref, n_z - 1, z_sem.at[0])


def per_device(places, n_var, genotypes, col_mean, inv_scale, targets, probes, delta):
    n_zl, n_x, n_y, n_core = places
    n_samp = math.prod(places)
    n_loc, m_loc = genotypes.shape
    groups, width = n_zl * n_x, n_y * LANES
    n_z = n_var * n_zl
    f32 = jnp.float32
    vmem = pl.BlockSpec(memory_space=pltpu.VMEM)
    dma = pltpu.SemaphoreType.DMA
    sol, assoc = pl.pallas_call(
        functools.partial(kernel, places, n_var, n_loc * n_samp, m_loc * n_var),
        out_shape=(
            jax.ShapeDtypeStruct((COLS, n_loc), f32),
            jax.ShapeDtypeStruct((m_loc // LANES, 1, LANES), f32),
        ),
        in_specs=[pl.BlockSpec(memory_space=pl.ANY)] + [vmem] * 4 + [pl.BlockSpec(memory_space=pltpu.SMEM)],
        out_specs=(vmem, vmem),
        scratch_shapes=[
            pltpu.VMEM((groups, n_loc, width), jnp.bfloat16),
            pltpu.VMEM((COLS, n_loc), f32),
            pltpu.VMEM((n_samp, COLS // n_core, LANES), f32),
            pltpu.VMEM((n_samp, COLS // n_core, LANES), f32),
            pltpu.VMEM((n_samp, COLS // n_core, LANES), f32),
            pltpu.VMEM((n_var, COLS, n_loc), f32),
            pltpu.VMEM((n_samp, COLS // n_core, LANES), f32),
            pltpu.VMEM((n_samp, COLS // n_core, LANES), f32),
            pltpu.VMEM((n_samp, 2, LANES), f32),
            pltpu.VMEM((n_z, 1, LANES), f32),
            dma((groups,)),
            dma((2,)),
            dma((2,)),
            dma,
            dma((groups,)),
            dma((2,)),
            dma,
            dma((n_zl,)),
            dma((2,)),
        ],
        compiler_params=pltpu.CompilerParams(
            collective_id=0, has_side_effects=True, vmem_limit_bytes=60 * 1024 * 1024
        ),
    )(
        genotypes,
        col_mean.reshape(groups, 1, width),
        inv_scale.reshape(groups, 1, width),
        targets.reshape(1, n_loc),
        probes.T,
        delta,
    )
    return sol.T, assoc.reshape(m_loc)


def solution(mesh):
    places = PLACES
    if math.prod(places) != mesh.shape["samp"]:
        raise ValueError("samp size")
    placed = (P("samp", "var"), P("var"), P("var"), P("samp"), P("samp", None), P())
    return jax.shard_map(
        functools.partial(per_device, places, mesh.shape["var"]),
        mesh=mesh,
        in_specs=placed,
        out_specs=(P("samp", None), P("var")),
        check_vma=False,
    )
```

time: 180 us -> 56.2 us (0.31)
  blocking collectives: 58.3 us -> 0 us
  Pallas kernels: 0 us -> 51.9 us
  starting transfers between devices: 39.9 us -> 0 us
  matrix products: 35.7 us -> 0 us
  waiting for transfers between devices: 25.4 us -> 0 us
  other arithmetic: 9.81 us -> 0 us
  local copies, waits for them, and re-layouts: 8.61 us -> 2.7 us
    all_to_all x4 -> x0, blocking collectives: 58.3 us -> none  [from_everyone(): lax.all_to_all(jnp.broadcast_to(shard[None], (count, *shard.shape)), axis...]
    pallas_call x0 -> x1, Pallas kernels: none -> 51.9 us  [per_device(): pl.pallas_call(functools.partial(kernel, places, n_var, n_loc * n_samp, m...]
    all_to_all x5 -> x0, starting transfers between devices: 39.9 us -> none  [the longest x3 24.1 us: from_everyone(): lax.all_to_all(jnp.broadcast_to(shard[None], (count, *shard.shape)), axis...]
    dot_general x7 -> x0, matrix products: 35.7 us -> none  [the longest x2 17.9 us: per_device(): jnp.dot(dense, scaled, precision=HI, preferred_element_type=jnp.float32)]
    all_to_all x5 -> x0, waiting for transfers between devices: 25.4 us -> none  [the longest x2 16.5 us: sent_and_summed(): lax.all_to_all(tiles, axis, split_axis=0, concat_axis=0, tiled=True)]
    all_to_all x4 -> x0, other arithmetic: 3.8 us -> none  [the longest x2 1.9 us: from_everyone(): lax.all_to_all(jnp.broadcast_to(shard[None], (count, *shard.shape)), axis...]
    reduce_sum x12 -> x0, other arithmetic: 3.42 us -> none  [the longest x2 1.16 us: across(): totals = jnp.sum(vectors, 0)]
    broadcast_in_dim x5 -> x0, local copies, waits for them, and re-layouts: 2.63 us -> none  [from_everyone(): jnp.broadcast_to(shard[None], (count, *shard.shape))]
  transfers between devices with their start and end apart: 5 -> 0, of which waited for: 5 -> 0; matrix products, arithmetic and copies ran while one was open for 8% -> 0% of each run, Pallas kernels for 0% -> 0%
where the time goes in v1:
time: 56.2 us; the launch traced here: 55.9 us
  Pallas kernels  51.9 us (92%)
  local copies, waits for them, and re-layouts  2.7 us (5%)
  between operations  1.29 us (2%)
    pallas_call x1, Pallas kernels, per_device(): pl.pallas_call(functools.partial(kernel, places, n_var, n_loc * n_samp, m...  51.9 us
    unnamed x2, local copies, waits for them, and re-layouts  2.7 us

profile of v1, /device:TPU:1, one launch (start us, length us, event | category | flops | bytes accessed | tf_op | source)
XLA Modules:
  0.0 55.9 jit_solution(13247151108289304707)
XLA Ops:
  1.3 51.9 %shard_map.77 = (f32[8,1024]{1,0:T(8,128)}, f32[32,1,128]{2,1,0:T(1,128)}) custom-call(bf16[1024,4096]{1,0:T(8,128)(2,1)} %g_hbm.1, f32[8,1,512]{2,1,0:T(1,128)} %bitcast.8, f32[8,1,512]{2,1,0:T(1,128)} %bitcast.9, f32[1,1024]{1,0:T(1,128)} %bitcast.11, f32[7,1024]{1,0:T(8,128)} %bitcast.6, f32[1]{0:T(128)S(6)} %copy.10.delta_ref), custom_call_target="tpu_custom_call" | custom-call | tf_op jit(solution)/shard_map/pallas_call | solution.py:240
  53.2 1.4 %copy.11 = f32[1024,8]{0,1:T(8,128)} copy(f32[1024,8]{0,1:T(8,128)} %bitcast.7) | data formatting | bytes 65536
  54.6 1.3 %copy.12 = f32[4096]{0:T(1024)} copy(f32[4096]{0:T(1024)} %bitcast.10) | data formatting | bytes 32768

commit v2 on v1

--- a/solution.py
+++ b/solution.py
@@ -12,12 +12,12 @@
 PLACES = (2, 4, 4, 2)
 COLS = 8
 LANES = 128
-
-
-def far(a, n):
-    if n == 4:
-        return lax.rem(2 + 3 * a + 3 * ((a * (a - 1)) // 2), 4)
-    return n - 1 - a
+AHEAD = 3
+HELD = 5
+
+
+def apart(d, n):
+    return min(d, n - d)
 
 
 def three(v):
@@ -34,10 +34,11 @@
 
 def kernel(
     places, n_var, n_total, m_total,
-    g_hbm, mean_ref, inv_ref, target_ref, probe_ref, delta_ref,
-    sol_ref, assoc_ref,
-    g_ref, rhs_ref, send1, recv1, c0_ref, part_ref, send2, recv2, sums_ref, z_ref,
-    g_sem, rs_send, rs_recv, ag_send, ag_recv, var_sem, sum_send, sum_recv, z_sem,
+    g_hbm, mean_hbm, inv_hbm, target_hbm, probe_hbm, delta_hbm,
+    sol_hbm, assoc_hbm,
+    g_ref, mean_ref, inv_ref, target_ref, probe_ref, delta_ref, sol_ref, assoc_ref,
+    rhs_ref, send1, recv1, c0_ref, part_ref, send2, recv2, sums_ref, z_ref,
+    g_sem, in_sem, out_sem, rs_send, rs_recv, ag_send, ag_recv, var_sem, sum_send, sum_recv, z_sem,
 ):
     n_zl, n_x, n_y, n_core = places
     n_samp = n_zl * n_x * n_y * n_core
@@ -56,22 +57,21 @@
     mine = me // members
     in_plane = lax.rem(me, plane)
     offsets = [(dz, dx) for dz in range(n_zl) for dx in range(n_x)]
-    near_first = sorted(offsets, key=lambda o: (o[0] + min(o[1], n_x - o[1]), o))
+    near_first = sorted(offsets, key=lambda o: (o[0] + apart(o[1], n_x), o))
     far_first = near_first[::-1]
-
-    def group_of(o):
-        return lax.rem(zl + o[0], n_zl) * n_x + lax.rem(x + o[1], n_x)
+    group_of = {o: lax.rem(zl + o[0], n_zl) * n_x + lax.rem(x + o[1], n_x) for o in offsets}
+    steps = sorted(((dy, dc) for dy in range(n_y) for dc in range(n_core)), key=lambda m: (-apart(m[0], n_y), -m[1]))
+    steps.remove((0, 0))
+    member_of = [lax.rem(y + dy, n_y) * n_core + lax.rem(core + dc, n_core) for dy, dc in steps + [(0, 0)]]
 
     def each_member(o, act):
-        group = group_of(o)
-
-        def one(k, carry):
-            ty = lax.rem(y + far(k // n_core, n_y), n_y)
-            tc = lax.rem(core + n_core - 1 - lax.rem(k, n_core), n_core)
-            act(group * members + ty * n_core + tc)
-            return carry
-
-        lax.fori_loop(0, members - (1 if o == (0, 0) else 0), one, 0)
+        first = group_of[o] * members
+        for k in range(members - (1 if o == (0, 0) else 0)):
+            act(first + member_of[k])
+
+    def on_line(d):
+        tz = lax.rem(z + d, n_z)
+        return lax.rem(tz, n_zl) * plane + in_plane, tz // n_zl
 
     def to(src, dst, send, recv, samp, var):
         pltpu.make_async_remote_copy(
@@ -86,57 +86,71 @@
         columns = pl.ds(pl.multiple_of(group * width, width), width)
         return pltpu.make_async_copy(g_hbm.at[:, columns], g_ref.at[group], g_sem.at[i])
 
-    for i, o in enumerate(far_first):
-        block(i, group_of(o)).start()
+    taken = [
+        pltpu.make_async_copy(src, dst, in_sem.at[i])
+        for i, (src, dst) in enumerate([
+            (target_hbm, target_ref), (probe_hbm, probe_ref), (mean_hbm, mean_ref), (inv_hbm, inv_ref),
+            (delta_hbm, delta_ref),
+        ])
+    ]
+    for copy in taken:
+        copy.start()
+    for i in range(AHEAD):
+        block(i, group_of[far_first[i]]).start()
 
     barrier = pltpu.get_barrier_semaphore()
 
-    def greet(k, carry):
-        pl.semaphore_signal(barrier, inc=1, device_id=(lax.rem(me + k, n_samp), va), device_id_type=MESH)
-        return carry
-
-    lax.fori_loop(1, n_samp, greet, 0)
-
-    def on_line(d):
-        tz = lax.rem(z + d, n_z)
-        return lax.rem(tz, n_zl) * plane + in_plane, tz // n_zl
-
+    def greet(samp, var):
+        pl.semaphore_signal(barrier, inc=1, device_id=(samp, var), device_id_type=MESH)
+
+    for o in far_first:
+        each_member(o, lambda t: greet(t, va))
     for d in range(1, n_z):
-        pl.semaphore_signal(barrier, inc=1, device_id=on_line(d), device_id_type=MESH)
+        greet(*on_line(d))
+
+    for copy in taken:
+        copy.wait()
 
     rhs_ref[0:1, :] = target_ref[...]
     rhs_ref[1:COLS, :] = probe_ref[...]
     rhs = rhs_ref[...]
 
-    def reduced(vec, send, recv, sem, first):
+    def reduced(vec, send, recv, sem, first, meanwhile):
         pieces = three(vec)
         total = jnp.sum(vec, 1, keepdims=True)
-        before = None
+
+        def send_group(o):
+            each_member(o, lambda t: to(send.at[t], recv.at[me], rs_send.at[sem], rs_recv.at[sem], t, va))
+
         for i, o in enumerate(far_first):
-            group = group_of(o)
+            group = group_of[o]
             if first:
                 block(i, group).wait()
+                if i + AHEAD < len(far_first):
+                    block(i + AHEAD, group_of[far_first[i + AHEAD]]).start()
             p = folded(jnp.dot(pieces, g_ref[group], preferred_element_type=jnp.float32))
             p = p - total * mean_ref[group]
+            held = min(HELD, len(far_first) - 1) if first else 1
+            if first and i == held:
+                pl.semaphore_wait(barrier, n_samp - 1 + n_z - 1)
+            if i == held:
+                for k in range(i):
+                    send_group(far_first[k])
+            elif i > held:
+                send_group(far_first[i - 1])
             for ky in range(n_y):
                 for kc in range(n_core):
                     send[group * members + ky * n_core + kc] = p[
                         kc * half : (kc + 1) * half, ky * LANES : (ky + 1) * LANES
                     ]
-            if first and i == 0:
-                pl.semaphore_wait(barrier, n_samp - 1 + n_z - 1)
-            if before is not None:
-                each_member(
-                    before, lambda t: to(send.at[t], recv.at[me], rs_send.at[sem], rs_recv.at[sem], t, va)
-                )
-            before = o
-        each_member(before, lambda t: to(send.at[t], recv.at[me], rs_send.at[sem], rs_recv.at[sem], t, va))
+        send_group(far_first[-1])
         recv[me] = send[me]
+        done = meanwhile()
         arrived(recv, n_samp - 1, rs_recv.at[sem])
         scale = inv_ref[mine, :, pl.ds(pl.multiple_of(y * LANES, LANES), LANES)]
-        return jnp.sum(recv[...], 0) * scale
-
-    share0 = reduced(rhs, send1, recv1, 0, True)
+        return jnp.sum(recv[...], 0) * scale, done
+
+    share0, _ = reduced(rhs, send1, recv1, 0, True, lambda: None)
     c0_ref[me] = share0
     for o in far_first:
         each_member(o, lambda t: to(c0_ref.at[me], c0_ref.at[me], ag_send, ag_recv.at[mine], t, va))
@@ -144,7 +158,7 @@
     rows = None
     shift = None
     for o in near_first:
-        group = group_of(o)
+        group = group_of[o]
         arrived(c0_ref, members - (1 if o == (0, 0) else 0), ag_recv.at[group])
         blocks = []
         for ky in range(n_y):
@@ -167,26 +181,25 @@
         image = image + part_ref[k]
     image = image * (1.0 / m_total)
 
-    share1 = reduced(image, send2, recv2, 1, False)
-
     row = lax.broadcasted_iota(jnp.int32, (COLS, LANES), 0)
     lane = lax.broadcasted_iota(jnp.int32, (COLS, LANES), 1)
     own = row // half == core
 
+    def put(spread, k, q):
+        return jnp.where(lane == row + COLS * k, jnp.sum(q, 1, keepdims=True), spread)
+
     def by_column(a):
-        spread = jnp.where(own, jnp.concatenate([a] * n_core, 0), 0.0)
-        return jnp.sum(spread, 1, keepdims=True)
-
-    def by_sample(a):
-        return jnp.sum(a, 1, keepdims=True) * (1.0 / n_var)
-
-    found = [
-        by_column(share0 * share0), by_column(share0 * share1), by_column(share1 * share1),
-        by_sample(rhs * rhs), by_sample(rhs * image), by_sample(image * image),
-    ]
-    spread = jnp.zeros((COLS, LANES), jnp.float32)
-    for k, q in enumerate(found):
-        spread = jnp.where(lane == row + COLS * k, q, spread)
+        return jnp.where(own, jnp.concatenate([a] * n_core, 0), 0.0)
+
+    def known():
+        spread = put(jnp.zeros((COLS, LANES), jnp.float32), 0, by_column(share0 * share0))
+        for k, (a, b) in enumerate([(rhs, rhs), (rhs, image), (image, image)]):
+            spread = put(spread, 3 + k, a * b * (1.0 / n_var))
+        return spread
+
+    share1, spread = reduced(image, send2, recv2, 1, False, known)
+    spread = put(spread, 1, by_column(share0 * share1))
+    spread = put(spread, 2, by_column(share1 * share1))
     sums_ref[me] = jnp.concatenate([jnp.sum(spread, 0, keepdims=True), share1[0:1, :]], 0)
     for o in sorted(far_first, key=lambda o: o[0]):
         each_member(o, lambda t: to(sums_ref.at[me], sums_ref.at[me], sum_send, sum_recv.at[zl], t, va))
@@ -199,7 +212,7 @@
     arrived(z_ref, n_z - 1, z_sem.at[1])
     every = jnp.broadcast_to(jnp.sum(z_ref[...], 0), (COLS, LANES))
     cc, cw, ww, rr, ri, ii = [
-        jnp.sum(jnp.where(lane == row + COLS * k, every, 0.0), 1, keepdims=True) for k in range(len(found))
+        jnp.sum(jnp.where(lane == row + COLS * k, every, 0.0), 1, keepdims=True) for k in range(6)
     ]
 
     delta = delta_ref[0]
@@ -213,6 +226,8 @@
     keep = alpha0 + alpha1 * lead
     less = alpha1 * alpha0
     sol_ref[...] = keep * rhs - less * image
+    sol_out = pltpu.make_async_copy(sol_ref, sol_hbm, out_sem.at[0])
+    sol_out.start()
     root = 1.0 / math.sqrt(n_total)
     keep_row = jnp.broadcast_to(keep[0:1, 0:1] * root, (1, LANES))
     less_row = jnp.broadcast_to(less[0:1, 0:1] * root, (1, LANES))
@@ -220,12 +235,16 @@
         at = q * n_core
         assoc_ref[q] = keep_row * c0_ref[at, 0:1, :] - less_row * sums_ref[at, 1:2, :]
 
+    assoc_out = pltpu.make_async_copy(assoc_ref, assoc_hbm, out_sem.at[1])
+    assoc_out.start()
     arrived(send1, n_samp - 1, rs_send.at[0])
     arrived(c0_ref, n_samp - 1, ag_send)
     arrived(part_ref, n_var - 1, var_sem.at[0])
     arrived(send2, n_samp - 1, rs_send.at[1])
     arrived(sums_ref, n_samp - 1, sum_send)
     arrived(z_ref, n_z - 1, z_sem.at[0])
+    sol_out.wait()
+    assoc_out.wait()
 
 
 def per_device(places, n_var, genotypes, col_mean, inv_scale, targets, probes, delta):
@@ -235,7 +254,7 @@
     groups, width = n_zl * n_x, n_y * LANES
     n_z = n_var * n_zl
     f32 = jnp.float32
-    vmem = pl.BlockSpec(memory_space=pltpu.VMEM)
+    hbm = pl.BlockSpec(memory_space=pltpu.HBM)
     dma = pltpu.SemaphoreType.DMA
     sol, assoc = pl.pallas_call(
         functools.partial(kernel, places, n_var, n_loc * n_samp, m_loc * n_var),
@@ -243,10 +262,17 @@
             jax.ShapeDtypeStruct((COLS, n_loc), f32),
             jax.ShapeDtypeStruct((m_loc // LANES, 1, LANES), f32),
         ),
-        in_specs=[pl.BlockSpec(memory_space=pl.ANY)] + [vmem] * 4 + [pl.BlockSpec(memory_space=pltpu.SMEM)],
-        out_specs=(vmem, vmem),
+        in_specs=[hbm] * 6,
+        out_specs=(hbm, hbm),
         scratch_shapes=[
             pltpu.VMEM((groups, n_loc, width), jnp.bfloat16),
+            pltpu.VMEM((groups, 1, width), f32),
+            pltpu.VMEM((groups, 1, width), f32),
+            pltpu.VMEM((1, n_loc), f32),
+            pltpu.VMEM((COLS - 1, n_loc), f32),
+            pltpu.SMEM((1,), f32),
+            pltpu.VMEM((COLS, n_loc), f32),
+            pltpu.VMEM((m_loc // LANES, 1, LANES), f32),
             pltpu.VMEM((COLS, n_loc), f32),
             pltpu.VMEM((n_samp, COLS // n_core, LANES), f32),
             pltpu.VMEM((n_samp, COLS // n_core, LANES), f32),
@@ -257,6 +283,8 @@
             pltpu.VMEM((n_samp, 2, LANES), f32),
             pltpu.VMEM((n_z, 1, LANES), f32),
             dma((groups,)),
+            dma((5,)),
+            dma((2,)),
             dma((2,)),
             dma((2,)),
             dma,

time: 56.2 us -> 49.5 us (0.88)
  Pallas kernels: 51.9 us -> 45.3 us
    pallas_call x1, Pallas kernels: 51.9 us -> 45.3 us  [per_device(): pl.pallas_call(functools.partial(kernel, places, n_var, n_loc * n_samp, m...]
where the time goes in v2:
time: 49.5 us; the launch traced here: 49.3 us
  Pallas kernels  45.3 us (92%)
  local copies, waits for them, and re-layouts  2.7 us (5%)
  between operations  1.29 us (3%)
    pallas_call x1, Pallas kernels, per_device(): pl.pallas_call(functools.partial(kernel, places, n_var, n_loc * n_samp, m...  45.3 us
    unnamed x2, local copies, waits for them, and re-layouts  2.7 us

profile of v2, /device:TPU:1, one launch (start us, length us, event | category | flops | bytes accessed | tf_op | source)
XLA Modules:
  0.0 49.3 jit_solution(4347864345951276031)
XLA Ops:
  1.3 45.3 %shard_map.77 = (f32[8,1024]{1,0:T(8,128)}, f32[32,1,128]{2,1,0:T(1,128)}) custom-call(bf16[1024,4096]{1,0:T(8,128)(2,1)} %g_hbm.1, f32[8,1,512]{2,1,0:T(1,128)} %bitcast.8, f32[8,1,512]{2,1,0:T(1,128)} %bitcast.9, f32[1,1024]{1,0:T(1,128)} %bitcast.11, f32[7,1024]{1,0:T(8,128)} %bitcast.6, f32[1]{0:T(128)S(6)} %copy.10.delta_hbm), custom_call_target="tpu_custom_call" | custom-call | tf_op jit(solution)/shard_map/pallas_call | solution.py:259
  46.6 1.4 %copy.11 = f32[1024,8]{0,1:T(8,128)} copy(f32[1024,8]{0,1:T(8,128)} %bitcast.7) | data formatting | bytes 65536
  48.0 1.3 %copy.12 = f32[4096]{0:T(1024)} copy(f32[4096]{0:T(1024)} %bitcast.10) | data formatting | bytes 32768

commit v3 on v2

--- a/solution.py
+++ b/solution.py
@@ -37,8 +37,8 @@
     g_hbm, mean_hbm, inv_hbm, target_hbm, probe_hbm, delta_hbm,
     sol_hbm, assoc_hbm,
     g_ref, mean_ref, inv_ref, target_ref, probe_ref, delta_ref, sol_ref, assoc_ref,
-    rhs_ref, send1, recv1, c0_ref, part_ref, send2, recv2, sums_ref, z_ref,
-    g_sem, in_sem, out_sem, rs_send, rs_recv, ag_send, ag_recv, var_sem, sum_send, sum_recv, z_sem,
+    rhs_ref, send1, recv1, c0_ref, part_ref, send2, recv2, sums_ref, own_ref, all_ref, z_ref,
+    g_sem, in_sem, out_sem, rs_send, rs_recv, ag_send, ag_recv, var_sem, sum_send, sum_recv, all_send, all_recv,
 ):
     n_zl, n_x, n_y, n_core = places
     n_samp = n_zl * n_x * n_y * n_core
@@ -46,16 +46,13 @@
     members = n_y * n_core
     half = COLS // n_core
     width = n_y * LANES
-    n_z = n_var * n_zl
     me = lax.axis_index("samp")
     va = lax.axis_index("var")
     core = lax.rem(me, n_core)
     y = lax.rem(me // n_core, n_y)
     x = lax.rem(me // members, n_x)
     zl = me // plane
-    z = va * n_zl + zl
     mine = me // members
-    in_plane = lax.rem(me, plane)
     offsets = [(dz, dx) for dz in range(n_zl) for dx in range(n_x)]
     near_first = sorted(offsets, key=lambda o: (o[0] + apart(o[1], n_x), o))
     far_first = near_first[::-1]
@@ -68,10 +65,6 @@
         first = group_of[o] * members
         for k in range(members - (1 if o == (0, 0) else 0)):
             act(first + member_of[k])
-
-    def on_line(d):
-        tz = lax.rem(z + d, n_z)
-        return lax.rem(tz, n_zl) * plane + in_plane, tz // n_zl
 
     def to(src, dst, send, recv, samp, var):
         pltpu.make_async_remote_copy(
@@ -103,10 +96,12 @@
     def greet(samp, var):
         pl.semaphore_signal(barrier, inc=1, device_id=(samp, var), device_id_type=MESH)
 
-    for o in far_first:
-        each_member(o, lambda t: greet(t, va))
-    for d in range(1, n_z):
-        greet(*on_line(d))
+    others = [(o, k, o[0] + apart(o[1], n_x) + apart(m[0], n_y)) for o in offsets for k, m in enumerate(steps)]
+    others += [(o, members - 1, o[0] + apart(o[1], n_x)) for o in offsets if o != (0, 0)]
+    peers = [(hops, group_of[o] * members + member_of[k], va) for o, k, hops in others]
+    peers += [(n_zl * apart(d, n_var), me, lax.rem(va + d, n_var)) for d in range(1, n_var)]
+    for _, samp, var in sorted(peers, key=lambda p: -p[0]):
+        greet(samp, var)
 
     for copy in taken:
         copy.wait()
@@ -132,7 +127,7 @@
             p = p - total * mean_ref[group]
             held = min(HELD, len(far_first) - 1) if first else 1
             if first and i == held:
-                pl.semaphore_wait(barrier, n_samp - 1 + n_z - 1)
+                pl.semaphore_wait(barrier, n_samp - 1 + n_var - 1)
             if i == held:
                 for k in range(i):
                     send_group(far_first[k])
@@ -157,21 +152,25 @@
 
     rows = None
     shift = None
-    for o in near_first:
-        group = group_of[o]
-        arrived(c0_ref, members - (1 if o == (0, 0) else 0), ag_recv.at[group])
-        blocks = []
-        for ky in range(n_y):
-            blocks.append(
-                jnp.concatenate([c0_ref[group * members + ky * n_core + kc] for kc in range(n_core)], 0)
+    rings = sorted({o[0] + apart(o[1], n_x) for o in offsets})
+    stages = [[o for o in near_first if o[0] + apart(o[1], n_x) == r] for r in rings]
+    for stage in stages:
+        for o in stage:
+            arrived(c0_ref, members - (1 if o == (0, 0) else 0), ag_recv.at[group_of[o]])
+        for o in stage:
+            group = group_of[o]
+            blocks = []
+            for ky in range(n_y):
+                blocks.append(
+                    jnp.concatenate([c0_ref[group * members + ky * n_core + kc] for kc in range(n_core)], 0)
+                )
+            scaled = jnp.concatenate(blocks, 1) * inv_ref[group]
+            off = jnp.sum(scaled * mean_ref[group], 1, keepdims=True)
+            p = lax.dot_general(
+                three(scaled), g_ref[group], (((1,), (1,)), ((), ())), preferred_element_type=jnp.float32
             )
-        scaled = jnp.concatenate(blocks, 1) * inv_ref[group]
-        off = jnp.sum(scaled * mean_ref[group], 1, keepdims=True)
-        p = lax.dot_general(
-            three(scaled), g_ref[group], (((1,), (1,)), ((), ())), preferred_element_type=jnp.float32
-        )
-        rows = p if rows is None else rows + p
-        shift = off if shift is None else shift + off
+            rows = p if rows is None else rows + p
+            shift = off if shift is None else shift + off
     part_ref[va] = folded(rows) - shift
     for d in sorted(range(1, n_var), key=lambda d: -min(d, n_var - d)):
         to(part_ref.at[va], part_ref.at[va], var_sem.at[0], var_sem.at[1], me, lax.rem(va + d, n_var))
@@ -201,15 +200,28 @@
     spread = put(spread, 1, by_column(share0 * share1))
     spread = put(spread, 2, by_column(share1 * share1))
     sums_ref[me] = jnp.concatenate([jnp.sum(spread, 0, keepdims=True), share1[0:1, :]], 0)
-    for o in sorted(far_first, key=lambda o: o[0]):
-        each_member(o, lambda t: to(sums_ref.at[me], sums_ref.at[me], sum_send, sum_recv.at[zl], t, va))
-    arrived(sums_ref, plane - 1, sum_recv.at[zl])
-    z_ref[z] = jnp.sum(sums_ref[pl.ds(zl * plane, plane)], 0)[0:1, :]
-    for d in sorted(range(1, n_z), key=lambda d: -min(d, n_z - d)):
-        to(z_ref.at[z], z_ref.at[z], z_sem.at[0], z_sem.at[1], *on_line(d))
-    for other in range(1, n_zl):
-        arrived(sums_ref, plane, sum_recv.at[lax.rem(zl + other, n_zl)])
-    arrived(z_ref, n_z - 1, z_sem.at[1])
+    own_ref[0] = sums_ref[me, 0:1, :]
+    turns = sorted(range(1, n_var), key=lambda d: -apart(d, n_var))
+    for d in turns:
+        var = lax.rem(va + d, n_var)
+        slot = all_ref.at[va * n_samp + me]
+        for o in far_first:
+            for k in range(members):
+                to(own_ref.at[0], slot, all_send, all_recv.at[va], group_of[o] * members + member_of[k], var)
+    for o in far_first:
+        each_member(o, lambda t: to(sums_ref.at[me], sums_ref.at[me], sum_send, sum_recv, t, va))
+
+    def summed(var):
+        z_ref[var] = jnp.sum(all_ref[pl.ds(var * n_samp, n_samp)], 0)
+
+    arrived(sums_ref, n_samp - 1, sum_recv)
+    for t in range(n_samp):
+        all_ref[va * n_samp + t] = sums_ref[t, 0:1, :]
+    summed(va)
+    for d in turns[::-1]:
+        var = lax.rem(va + n_var - d, n_var)
+        arrived(all_ref, n_samp, all_recv.at[var])
+        summed(var)
     every = jnp.broadcast_to(jnp.sum(z_ref[...], 0), (COLS, LANES))
     cc, cw, ww, rr, ri, ii = [
         jnp.sum(jnp.where(lane == row + COLS * k, every, 0.0), 1, keepdims=True) for k in range(6)
@@ -242,9 +254,14 @@
     arrived(part_ref, n_var - 1, var_sem.at[0])
     arrived(send2, n_samp - 1, rs_send.at[1])
     arrived(sums_ref, n_samp - 1, sum_send)
-    arrived(z_ref, n_z - 1, z_sem.at[0])
+    arrived(all_ref, n_samp * (n_var - 1), all_send)
     sol_out.wait()
     assoc_out.wait()
+
+
+def handed_on(sol_in, assoc_in, sol_out, assoc_out):
+    sol_out[...] = sol_in[...]
+    assoc_out[...] = assoc_in[...]
 
 
 def per_device(places, n_var, genotypes, col_mean, inv_scale, targets, probes, delta):
@@ -252,7 +269,6 @@
     n_samp = math.prod(places)
     n_loc, m_loc = genotypes.shape
     groups, width = n_zl * n_x, n_y * LANES
-    n_z = n_var * n_zl
     f32 = jnp.float32
     hbm = pl.BlockSpec(memory_space=pltpu.HBM)
     dma = pltpu.SemaphoreType.DMA
@@ -281,7 +297,9 @@
             pltpu.VMEM((n_samp, COLS // n_core, LANES), f32),
             pltpu.VMEM((n_samp, COLS // n_core, LANES), f32),
             pltpu.VMEM((n_samp, 2, LANES), f32),
-            pltpu.VMEM((n_z, 1, LANES), f32),
+            pltpu.VMEM((1, 1, LANES), f32),
+            pltpu.VMEM((n_var * n_samp, 1, LANES), f32),
+            pltpu.VMEM((n_var, 1, LANES), f32),
             dma((groups,)),
             dma((5,)),
             dma((2,)),
@@ -291,8 +309,9 @@
             dma((groups,)),
             dma((2,)),
             dma,
-            dma((n_zl,)),
-            dma((2,)),
+            dma,
+            dma,
+            dma((n_var,)),
         ],
         compiler_params=pltpu.CompilerParams(
             collective_id=0, has_side_effects=True, vmem_limit_bytes=60 * 1024 * 1024
@@ -305,6 +324,12 @@
         probes.T,
         delta,
     )
+    sol, assoc = pl.pallas_call(
+        handed_on,
+        out_shape=(jax.ShapeDtypeStruct(sol.shape, f32), jax.ShapeDtypeStruct(assoc.shape, f32)),
+        in_specs=[pl.BlockSpec(memory_space=pltpu.VMEM)] * 2,
+        out_specs=(pl.BlockSpec(memory_space=pltpu.VMEM),) * 2,
+    )(sol, assoc)
     return sol.T, assoc.reshape(m_loc)
 
 

time: 49.5 us -> 47.8 us (0.966)
  local copies, waits for them, and re-layouts: 2.7 us -> 0 us
  Pallas kernels: 45.3 us -> 46.3 us
    unnamed x2 -> x0, local copies, waits for them, and re-layouts: 2.7 us -> none
    pallas_call x0 -> x1, Pallas kernels: none -> 1.38 us  [per_device(): pl.pallas_call(handed_on, out_shape=(jax.ShapeDtypeStruct(sol.shape, f32)...]
where the time goes in v3:
time: 47.8 us; the launch traced here: 47.6 us
  Pallas kernels  46.3 us (97%)
  between operations  1.29 us (3%)
    pallas_call x1, Pallas kernels, per_device(): pl.pallas_call(functools.partial(kernel, places, n_var, n_loc * n_samp, m...  44.9 us
    pallas_call x1, Pallas kernels, per_device(): pl.pallas_call(handed_on, out_shape=(jax.ShapeDtypeStruct(sol.shape, f32)...  1.38 us

profile of v3, /device:TPU:1, one launch (start us, length us, event | category | flops | bytes accessed | tf_op | source)
XLA Modules:
  0.0 47.6 jit_solution(12842823389706037269)
XLA Ops:
  1.3 44.9 %shard_map.77 = (f32[8,1024]{1,0:T(8,128)}, f32[32,1,128]{2,1,0:T(1,128)}) custom-call(bf16[1024,4096]{1,0:T(8,128)(2,1)} %g_hbm.1, f32[8,1,512]{2,1,0:T(1,128)} %bitcast.7, f32[8,1,512]{2,1,0:T(1,128)} %bitcast.8, f32[1,1024]{1,0:T(1,128)} %bitcast.9, f32[7,1024]{1,0:T(8,128)} %bitcast.6, f32[1]{0:T(128)S(6)} %copy.8.delta_hbm), custom_call_target="tpu_custom_call" | custom-call | tf_op jit(solution)/shard_map/pallas_call | solution.py:275
  46.2 1.4 %shard_map.78 = (f32[8,1024]{1,0:T(8,128)}, f32[32,1,128]{2,1,0:T(1,128)}) custom-call(f32[8,1024]{1,0:T(8,128)} %get-tuple-element.6.sol_in, f32[32,1,128]{2,1,0:T(1,128)} %get-tuple-element.7.assoc_in), custom_call_target="tpu_custom_call" | custom-call | tf_op jit(solution)/shard_map/pallas_call | solution.py:327

commit v4 on v3

--- a/solution.py
+++ b/solution.py
@@ -35,10 +35,10 @@
 def kernel(
     places, n_var, n_total, m_total,
     g_hbm, mean_hbm, inv_hbm, target_hbm, probe_hbm, delta_hbm,
-    sol_hbm, assoc_hbm,
-    g_ref, mean_ref, inv_ref, target_ref, probe_ref, delta_ref, sol_ref, assoc_ref,
+    sol_ref, assoc_ref,
+    g_ref, mean_ref, inv_ref, target_ref, probe_ref, delta_ref,
     rhs_ref, send1, recv1, c0_ref, part_ref, send2, recv2, sums_ref, own_ref, all_ref, z_ref,
-    g_sem, in_sem, out_sem, rs_send, rs_recv, ag_send, ag_recv, var_sem, sum_send, sum_recv, all_send, all_recv,
+    g_sem, in_sem, rs_send, rs_recv, ag_send, ag_recv, var_sem, sum_send, sum_recv, all_send, all_recv,
 ):
     n_zl, n_x, n_y, n_core = places
     n_samp = n_zl * n_x * n_y * n_core
@@ -238,8 +238,6 @@
     keep = alpha0 + alpha1 * lead
     less = alpha1 * alpha0
     sol_ref[...] = keep * rhs - less * image
-    sol_out = pltpu.make_async_copy(sol_ref, sol_hbm, out_sem.at[0])
-    sol_out.start()
     root = 1.0 / math.sqrt(n_total)
     keep_row = jnp.broadcast_to(keep[0:1, 0:1] * root, (1, LANES))
     less_row = jnp.broadcast_to(less[0:1, 0:1] * root, (1, LANES))
@@ -247,16 +245,12 @@
         at = q * n_core
         assoc_ref[q] = keep_row * c0_ref[at, 0:1, :] - less_row * sums_ref[at, 1:2, :]
 
-    assoc_out = pltpu.make_async_copy(assoc_ref, assoc_hbm, out_sem.at[1])
-    assoc_out.start()
     arrived(send1, n_samp - 1, rs_send.at[0])
     arrived(c0_ref, n_samp - 1, ag_send)
     arrived(part_ref, n_var - 1, var_sem.at[0])
     arrived(send2, n_samp - 1, rs_send.at[1])
     arrived(sums_ref, n_samp - 1, sum_send)
     arrived(all_ref, n_samp * (n_var - 1), all_send)
-    sol_out.wait()
-    assoc_out.wait()
 
 
 def handed_on(sol_in, assoc_in, sol_out, assoc_out):
@@ -271,15 +265,16 @@
     groups, width = n_zl * n_x, n_y * LANES
     f32 = jnp.float32
     hbm = pl.BlockSpec(memory_space=pltpu.HBM)
+    vmem = pl.BlockSpec(memory_space=pltpu.VMEM)
     dma = pltpu.SemaphoreType.DMA
     sol, assoc = pl.pallas_call(
         functools.partial(kernel, places, n_var, n_loc * n_samp, m_loc * n_var),
         out_shape=(
-            jax.ShapeDtypeStruct((COLS, n_loc), f32),
-            jax.ShapeDtypeStruct((m_loc // LANES, 1, LANES), f32),
+            pltpu.VMEM((COLS, n_loc), f32),
+            pltpu.VMEM((m_loc // LANES, 1, LANES), f32),
         ),
         in_specs=[hbm] * 6,
-        out_specs=(hbm, hbm),
+        out_specs=(vmem, vmem),
         scratch_shapes=[
             pltpu.VMEM((groups, n_loc, width), jnp.bfloat16),
             pltpu.VMEM((groups, 1, width), f32),
@@ -288,8 +283,6 @@
             pltpu.VMEM((COLS - 1, n_loc), f32),
             pltpu.SMEM((1,), f32),
             pltpu.VMEM((COLS, n_loc), f32),
-            pltpu.VMEM((m_loc // LANES, 1, LANES), f32),
-            pltpu.VMEM((COLS, n_loc), f32),
             pltpu.VMEM((n_samp, COLS // n_core, LANES), f32),
             pltpu.VMEM((n_samp, COLS // n_core, LANES), f32),
             pltpu.VMEM((n_samp, COLS // n_core, LANES), f32),
@@ -302,7 +295,6 @@
             pltpu.VMEM((n_var, 1, LANES), f32),
             dma((groups,)),
             dma((5,)),
-            dma((2,)),
             dma((2,)),
             dma((2,)),
             dma,
@@ -329,7 +321,7 @@
         out_shape=(jax.ShapeDtypeStruct(sol.shape, f32), jax.ShapeDtypeStruct(assoc.shape, f32)),
         in_specs=[pl.BlockSpec(memory_space=pltpu.VMEM)] * 2,
         out_specs=(pl.BlockSpec(memory_space=pltpu.VMEM),) * 2,
-    )(sol, assoc)
+    )(pltpu.with_memory_space_constraint(sol, pltpu.VMEM), pltpu.with_memory_space_constraint(assoc, pltpu.VMEM))
     return sol.T, assoc.reshape(m_loc)
 
 

time: 47.8 us -> 46.3 us (0.969)
  Pallas kernels: 46.3 us -> 44.9 us
    pallas_call x1, Pallas kernels: 1.38 us -> 0.62 us  [per_device(): pl.pallas_call(handed_on, out_shape=(jax.ShapeDtypeStruct(sol.shape, f32)...]
    pallas_call x1, Pallas kernels: 44.9 us -> 44.3 us  [per_device(): pl.pallas_call(functools.partial(kernel, places, n_var, n_loc * n_samp, m...]
where the time goes in v4:
time: 46.3 us; the launch traced here: 46.2 us
  Pallas kernels  44.9 us (97%)
  between operations  1.29 us (3%)
    pallas_call x1, Pallas kernels, per_device(): pl.pallas_call(functools.partial(kernel, places, n_var, n_loc * n_samp, m...  44.3 us

profile of v4, /device:TPU:1, one launch (start us, length us, event | category | flops | bytes accessed | tf_op | source)
XLA Modules:
  0.0 46.2 jit_solution(13642111300799647053)
XLA Ops:
  1.3 44.3 %shard_map.77 = (f32[8,1024]{1,0:T(8,128)S(1)}, f32[32,1,128]{2,1,0:T(1,128)S(1)}) custom-call(bf16[1024,4096]{1,0:T(8,128)(2,1)} %g_hbm.1, f32[8,1,512]{2,1,0:T(1,128)} %bitcast.7, f32[8,1,512]{2,1,0:T(1,128)} %bitcast.8, f32[1,1024]{1,0:T(1,128)} %bitcast.9, f32[7,1024]{1,0:T(8,128)} %bitcast.6, f32[1]{0:T(128)S(6)} %copy.8.delta_hbm), custom_call_target="tpu_custom_call" | custom-call | tf_op jit(solution)/shard_map/pallas_call | solution.py:270
  45.6 0.6 %shard_map.78 = (f32[8,1024]{1,0:T(8,128)}, f32[32,1,128]{2,1,0:T(1,128)}) custom-call(f32[8,1024]{1,0:T(8,128)S(1)} %get-tuple-element.6.sol_in, f32[32,1,128]{2,1,0:T(1,128)S(1)} %get-tuple-element.7.assoc_in), custom_call_target="tpu_custom_call" | custom-call | tf_op jit(solution)/shard_map/pallas_call | solution.py:319

commit v5 on v4

--- a/solution.py
+++ b/solution.py
@@ -12,6 +12,7 @@
 PLACES = (2, 4, 4, 2)
 COLS = 8
 LANES = 128
+CUTS = (1, 4, 7)
 AHEAD = 3
 HELD = 5
 
@@ -20,16 +21,14 @@
     return min(d, n - d)
 
 
-def three(v):
+def two(v):
     high = v.astype(jnp.bfloat16).astype(jnp.float32)
-    rest = v - high
-    mid = rest.astype(jnp.bfloat16).astype(jnp.float32)
-    low = rest - mid
-    return jnp.concatenate([high, mid, low], 0).astype(jnp.bfloat16)
+    low = (v - high).astype(jnp.bfloat16).astype(jnp.float32)
+    return jnp.concatenate([high, low], 0).astype(jnp.bfloat16), high + low
 
 
 def folded(p):
-    return p[0:COLS] + p[COLS : 2 * COLS] + p[2 * COLS : 3 * COLS]
+    return p[0:COLS] + p[COLS : 2 * COLS]
 
 
 def kernel(
@@ -111,34 +110,47 @@
     rhs = rhs_ref[...]
 
     def reduced(vec, send, recv, sem, first, meanwhile):
-        pieces = three(vec)
-        total = jnp.sum(vec, 1, keepdims=True)
+        pieces, whole = two(vec)
+        total = jnp.sum(whole, 1, keepdims=True)
 
         def send_group(o):
             each_member(o, lambda t: to(send.at[t], recv.at[me], rs_send.at[sem], rs_recv.at[sem], t, va))
 
-        for i, o in enumerate(far_first):
-            group = group_of[o]
-            if first:
-                block(i, group).wait()
+        def product(o):
+            p = folded(jnp.dot(pieces, g_ref[group_of[o]], preferred_element_type=jnp.float32))
+            return p - total * mean_ref[group_of[o]]
+
+        def store(o, p):
+            for ky in range(n_y):
+                for kc in range(n_core):
+                    send[group_of[o] * members + ky * n_core + kc] = p[
+                        kc * half : (kc + 1) * half, ky * LANES : (ky + 1) * LANES
+                    ]
+
+        held = min(HELD, len(far_first) - 1)
+        if first:
+            for i, o in enumerate(far_first):
+                block(i, group_of[o]).wait()
                 if i + AHEAD < len(far_first):
                     block(i + AHEAD, group_of[far_first[i + AHEAD]]).start()
-            p = folded(jnp.dot(pieces, g_ref[group], preferred_element_type=jnp.float32))
-            p = p - total * mean_ref[group]
-            held = min(HELD, len(far_first) - 1) if first else 1
-            if first and i == held:
-                pl.semaphore_wait(barrier, n_samp - 1 + n_var - 1)
-            if i == held:
-                for k in range(i):
-                    send_group(far_first[k])
-            elif i > held:
-                send_group(far_first[i - 1])
-            for ky in range(n_y):
-                for kc in range(n_core):
-                    send[group * members + ky * n_core + kc] = p[
-                        kc * half : (kc + 1) * half, ky * LANES : (ky + 1) * LANES
-                    ]
-        send_group(far_first[-1])
+                p = product(o)
+                if i == held:
+                    pl.semaphore_wait(barrier, n_samp - 1 + n_var - 1)
+                    for k in range(i):
+                        send_group(far_first[k])
+                elif i > held:
+                    send_group(far_first[i - 1])
+                store(o, p)
+            send_group(far_first[-1])
+        else:
+            cuts = [c for c in CUTS if c < len(far_first)] + [len(far_first)]
+            for lo, hi in zip([0] + cuts, cuts):
+                stage = far_first[lo:hi]
+                done = [product(o) for o in stage]
+                for o, p in zip(stage, done):
+                    store(o, p)
+                for o in stage:
+                    send_group(o)
         recv[me] = send[me]
         done = meanwhile()
         arrived(recv, n_samp - 1, rs_recv.at[sem])
@@ -165,9 +177,10 @@
                     jnp.concatenate([c0_ref[group * members + ky * n_core + kc] for kc in range(n_core)], 0)
                 )
             scaled = jnp.concatenate(blocks, 1) * inv_ref[group]
-            off = jnp.sum(scaled * mean_ref[group], 1, keepdims=True)
+            pieces, whole = two(scaled)
+            off = jnp.sum(whole * mean_ref[group], 1, keepdims=True)
             p = lax.dot_general(
-                three(scaled), g_ref[group], (((1,), (1,)), ((), ())), preferred_element_type=jnp.float32
+                pieces, g_ref[group], (((1,), (1,)), ((), ())), preferred_element_type=jnp.float32
             )
             rows = p if rows is None else rows + p
             shift = off if shift is None else shift + off
@@ -202,14 +215,20 @@
     sums_ref[me] = jnp.concatenate([jnp.sum(spread, 0, keepdims=True), share1[0:1, :]], 0)
     own_ref[0] = sums_ref[me, 0:1, :]
     turns = sorted(range(1, n_var), key=lambda d: -apart(d, n_var))
-    for d in turns:
-        var = lax.rem(va + d, n_var)
-        slot = all_ref.at[va * n_samp + me]
-        for o in far_first:
-            for k in range(members):
-                to(own_ref.at[0], slot, all_send, all_recv.at[va], group_of[o] * members + member_of[k], var)
-    for o in far_first:
-        each_member(o, lambda t: to(sums_ref.at[me], sums_ref.at[me], sum_send, sum_recv, t, va))
+    slot = all_ref.at[va * n_samp + me]
+    along = {d: lax.rem(va + n_var + (1 - 2 * zl) * d, n_var) for d in turns}
+    every_one = []
+    for o in offsets:
+        for k, m in enumerate(steps + [(0, 0)]):
+            flat = apart(o[1], n_x) + apart(m[0], n_y)
+            every_one += [(apart(d * n_zl + o[0], n_var * n_zl) + flat, o, k, d) for d in range(n_var)]
+    every_one.remove((0, (0, 0), members - 1, 0))
+    for _, o, k, d in sorted(every_one, key=lambda e: -e[0]):
+        samp = group_of[o] * members + member_of[k]
+        if d:
+            to(own_ref.at[0], slot, all_send, all_recv.at[va], samp, along[d])
+        else:
+            to(sums_ref.at[me], sums_ref.at[me], sum_send, sum_recv, samp, va)
 
     def summed(var):
         z_ref[var] = jnp.sum(all_ref[pl.ds(var * n_samp, n_samp)], 0)

time: 46.3 us -> 45.3 us (0.978)
  Pallas kernels: 44.9 us -> 43.9 us
    pallas_call x1, Pallas kernels: 44.3 us -> 43.3 us  [per_device(): pl.pallas_call(functools.partial(kernel, places, n_var, n_loc * n_samp, m...]
where the time goes in v5:
time: 45.3 us; the launch traced here: 45.2 us
  Pallas kernels  43.9 us (97%)
  between operations  1.29 us (3%)
    pallas_call x1, Pallas kernels, per_device(): pl.pallas_call(functools.partial(kernel, places, n_var, n_loc * n_samp, m...  43.3 us

profile of v5, /device:TPU:1, one launch (start us, length us, event | category | flops | bytes accessed | tf_op | source)
XLA Modules:
  0.0 45.2 jit_solution(14532679755400331559)
XLA Ops:
  1.3 43.3 %shard_map.77 = (f32[8,1024]{1,0:T(8,128)S(1)}, f32[32,1,128]{2,1,0:T(1,128)S(1)}) custom-call(bf16[1024,4096]{1,0:T(8,128)(2,1)} %g_hbm.1, f32[8,1,512]{2,1,0:T(1,128)} %bitcast.7, f32[8,1,512]{2,1,0:T(1,128)} %bitcast.8, f32[1,1024]{1,0:T(1,128)} %bitcast.9, f32[7,1024]{1,0:T(8,128)} %bitcast.6, f32[1]{0:T(128)S(6)} %copy.8.delta_hbm), custom_call_target="tpu_custom_call" | custom-call | tf_op jit(solution)/shard_map/pallas_call | solution.py:289
  44.6 0.6 %shard_map.78 = (f32[8,1024]{1,0:T(8,128)}, f32[32,1,128]{2,1,0:T(1,128)}) custom-call(f32[8,1024]{1,0:T(8,128)S(1)} %get-tuple-element.6.sol_in, f32[32,1,128]{2,1,0:T(1,128)S(1)} %get-tuple-element.7.assoc_in), custom_call_target="tpu_custom_call" | custom-call | tf_op jit(solution)/shard_map/pallas_call | solution.py:338
